TPU v7x, 32 devices: a whole 2x2x4 slice. The times are simulated.
32 devices in a mesh: mem: 8 (over y, x, core), grid: 4 (over z).
Axes of the slice: x: 2, y: 2, z: 4, core: 2. Of those that a mesh axis runs over, the one named last changes fastest.
Arguments:
- ensemble: bfloat16 [16, 4, 128, 8, 128], P('mem', None, None, 'grid'), may hold values from -6 to 6
- control: bfloat16 [16, 128, 8, 128], P('mem', None, 'grid'), may hold values from -6 to 6
- vertical: bfloat16 [128, 128], replicated, may hold values from -0.5 to 0.5
- inverse_var: float32 [4, 128], replicated, may hold values from 0.25 to 4
- obs_code: int32 [16, 256], P('grid'), may hold values from 0 to 4
- obs_count: int32 [16, 256], P('grid'), may hold values from 0 to 3
Outputs:
- product: float32 [16, 128, 8, 128], P('mem', None, 'grid')
All inputs are finite; a program needn't handle non-finite values.
Results may differ from a plain program's by a relative error of at most 0.00045.
Values sent between devices are 32-bit elements; how exact they have to be, the bound alone decides.
A program may use at most 64 MiB of HBM per device.

v0:
```python
import jax
import jax.numpy as jnp
from jax import lax
from jax.sharding import PartitionSpec as P

diffusion = 0.2
near_weight = 0.75
far_weight = 0.25


def with_halo(block, sides, width):
    for axis, dim in sides:
        count = lax.axis_size(axis)
        forward = [(i, i + 1) for i in range(count - 1)]
        backward = [(target, source) for source, target in forward]
        low = lax.ppermute(
            lax.slice_in_dim(block, block.shape[dim] - width, None, axis=dim), axis, forward
        )
        high = lax.ppermute(lax.slice_in_dim(block, 0, width, axis=dim), axis, backward)
        block = jnp.concatenate([low, block, high], axis=dim)
    return block


def shifted(shard, axis, by):
    size = lax.axis_size(axis)
    pairs = [(i, i + by) for i in range(size) if 0 <= i + by < size]
    return lax.ppermute(shard, axis, pairs)


def column_pair(field):
    padded = jnp.pad(field, [(0, 0)] * (field.ndim - 1) + [(1, 1)])
    return padded[..., 2:] + padded[..., :-2]


def smooth_rows(extended):
    center = extended[..., 1:-1, :]
    return center + diffusion * (
        extended[..., 2:, :] + extended[..., :-2, :] + column_pair(center) - 4.0 * center
    )


def refine(coarse, extended):
    upper = near_weight * coarse + far_weight * extended[..., :-2, :]
    lower = near_weight * coarse + far_weight * extended[..., 2:, :]
    rows_fine = jnp.stack([upper, lower], axis=-2)
    rows_fine = rows_fine.reshape(coarse.shape[:-2] + (2 * coarse.shape[-2], coarse.shape[-1]))
    padded = jnp.pad(rows_fine, [(0, 0)] * (rows_fine.ndim - 1) + [(1, 1)])
    left = near_weight * rows_fine + far_weight * padded[..., :-2]
    right = near_weight * rows_fine + far_weight * padded[..., 2:]
    both = jnp.stack([left, right], axis=-1)
    return both.reshape(rows_fine.shape[:-1] + (2 * rows_fine.shape[-1],))


def coarsen(fine_field, extended):
    half_rows = fine_field.shape[-2] // 2
    rows_coarse = near_weight * (fine_field[..., 0::2, :] + fine_field[..., 1::2, :])
    rows_coarse = rows_coarse + far_weight * (
        extended[..., 0 : 2 * half_rows : 2, :] + extended[..., 3::2, :]
    )
    width = rows_coarse.shape[-1]
    padded = jnp.pad(rows_coarse, [(0, 0)] * (rows_coarse.ndim - 1) + [(1, 1)])
    result = near_weight * (rows_coarse[..., 0::2] + rows_coarse[..., 1::2])
    return result + far_weight * (padded[..., 0:width:2] + padded[..., 3::2])


def obs_masks(code):
    return [(code == which).astype(jnp.float32) for which in range(1, 5)]


def observe(fine_field, extended, masks, count, weights):
    padded = jnp.pad(fine_field, [(0, 0)] * (fine_field.ndim - 1) + [(1, 1)])
    diff = fine_field - masks[0] * extended[..., 2:, :] - masks[1] * extended[..., :-2, :]
    diff = diff - masks[2] * padded[..., 2:] - masks[3] * padded[..., :-2]
    return count.astype(jnp.float32) * weights[:, :, None, None] * diff


def adjoint_rows(forcing, masks, above, below):
    first = masks[0] * forcing
    second = masks[1] * forcing
    from_above = jnp.concatenate([above, first[..., :-1, :]], axis=-2)
    from_below = jnp.concatenate([second[..., 1:, :], below], axis=-2)
    pad_spec = [(0, 0)] * (forcing.ndim - 1) + [(1, 1)]
    from_left = jnp.pad(masks[2] * forcing, pad_spec)[..., :-2]
    from_right = jnp.pad(masks[3] * forcing, pad_spec)[..., 2:]
    return forcing - from_above - from_below - from_left - from_right


def per_device(ensemble, control, vertical, inverse_var, obs_code, obs_count):
    member_count = ensemble.shape[0]
    factor = (member_count * lax.axis_size("mem")) ** (-0.5)

    def margin(field):
        return with_halo(field, (("grid", 2),), 1)

    def smooth_pair(field):
        first_pass = smooth_rows(margin(field))
        return smooth_rows(margin(first_pass))

    masks = obs_masks(obs_code)
    mixed = jnp.einsum("lm,kmxy->klxy", vertical, control, preferred_element_type=jnp.float32)
    local = smooth_pair(mixed)
    partial_value = jnp.zeros(ensemble.shape[1:], jnp.float32)
    for member in range(member_count):
        partial_value = partial_value + ensemble[member].astype(jnp.float32) * local[member][None]
    partial_value = factor * partial_value
    share = lax.psum_scatter(partial_value, "mem", scatter_dimension=1, tiled=True)
    level_count = share.shape[1]
    weights = lax.dynamic_slice_in_dim(
        inverse_var, lax.axis_index("mem") * level_count, level_count, 1
    )
    fine_field = refine(share, margin(share))
    forcing = observe(fine_field, margin(fine_field), masks, obs_count, weights)
    above = shifted((masks[0] * forcing)[:, :, -1:, :], "grid", 1)
    below = shifted((masks[1] * forcing)[:, :, :1, :], "grid", -1)
    adjoint_fine = adjoint_rows(forcing, masks, above, below)
    adjoint = lax.all_gather(coarsen(adjoint_fine, margin(adjoint_fine)), "mem", axis=1, tiled=True)
    projected = jnp.stack(
        [
            factor * jnp.sum(ensemble[member].astype(jnp.float32) * adjoint, axis=0)
            for member in range(member_count)
        ],
        axis=0,
    )
    rounded = smooth_pair(projected).astype(jnp.bfloat16)
    back = jnp.einsum("ml,kmxy->klxy", vertical, rounded, preferred_element_type=jnp.float32)
    return control.astype(jnp.float32) + back


def solution(mesh):
    return jax.shard_map(
        per_device,
        mesh=mesh,
        in_specs=(
            P("mem", None, None, "grid", None),
            P("mem", None, "grid", None),
            P(),
            P(),
            P("grid", None),
            P("grid", None),
        ),
        out_specs=P("mem", None, "grid", None),
        check_vma=False,
    )
```

profile of v0, /device:TPU:0, one launch (start us, length us, event | category | flops | bytes accessed | tf_op | source)
XLA Modules:
  0.0 151.9 jit_solution(7440111710614539400)
XLA Ops:
  9.2 5.6 %collective-permute-start.1 = (f32[2,128,1,128]{1,3,2,0:T(8,128)S(1)}, f32[2,128,1,128]{1,3,2,0:T(8,128)S(1)}, u32[]{:S(2)}, u32[]{:S(2)}) collective-permute-start(f32[2,128,1,128]{1,3,2,0:T(8,128)S(1)} %get-tuple-element.27), channel_id=1, source_target_pairs={{0,1},{1,2},{2,3},{4,5},{5,6},{6,7},{8,9},{9,10},{10,11},{12,13},{... | collective-permute-start | bytes 393224 | tf_op jit(solution)/shard_map/ppermute | solution.py:16
  14.8 1.6 %collective-permute-done = f32[2,128,1,128]{1,3,2,0:T(8,128)S(1)} collective-permute-done((f32[2,128,1,128]{1,3,2,0:T(8,128)S(1)}, f32[2,128,1,128]{1,3,2,0:T(8,128)S(1)}, u32[]{:S(2)}, u32[]{:S(2)}) %collective-permute-start) | collective-permute-done | bytes 131104 | tf_op jit(solution)/shard_map/ppermute | solution.py:19
  18.9 5.0 %collective-permute-start.3 = (f32[2,128,1,128]{1,3,2,0:T(8,128)S(1)}, f32[2,128,1,128]{1,3,2,0:T(8,128)S(1)}, u32[]{:S(2)}, u32[]{:S(2)}) collective-permute-start(f32[2,128,1,128]{1,3,2,0:T(8,128)S(1)} %get-tuple-element.25), channel_id=1, source_target_pairs={{0,1},{1,2},{2,3},{4,5},{5,6},{6,7},{8,9},{9,10},{10,11},{12,13},{... | collective-permute-start | bytes 393224 | tf_op jit(solution)/shard_map/ppermute | solution.py:16
  25.0 1.5 collective-permute-done.3
  27.7 37.0 %reduce-scatter.2.cloned.1.call-done = f32[4,16,2,128]{3,1,2,0:T(8,128)} async-done(((f32[4,128,2,128]{3,1,2,0:T(8,128)}), f32[4,16,2,128]{3,1,2,0:T(8,128)}) %reduce-scatter.2.cloned.1.call-update) | async-done | bytes 65552 | tf_op jit(solution)/shard_map/reduce_scatter | solution.py:106
  65.5 3.4 %collective-permute-start.4 = (f32[4,16,1,128]{3,1,2,0:T(8,128)S(1)}, f32[4,16,1,128]{3,1,2,0:T(8,128)S(1)}, u32[]{:S(2)}, u32[]{:S(2)}) collective-permute-start(f32[4,16,1,128]{3,1,2,0:T(8,128)S(1)} %get-tuple-element.32), channel_id=1, source_target_pairs={{0,1},{1,2},{2,3},{4,5},{5,6},{6,7},{8,9},{9,10},{10,11},{12,13},{... | collective-permute-start | bytes 98312 | tf_op jit(solution)/shard_map/ppermute | solution.py:16
  70.5 4.2 %collective-permute-done.5 = f32[4,16,1,128]{3,1,2,0:T(8,128)S(1)} collective-permute-done((f32[4,16,1,128]{3,1,2,0:T(8,128)S(1)}, f32[4,16,1,128]{3,1,2,0:T(8,128)S(1)}, u32[]{:S(2)}, u32[]{:S(2)}) %collective-permute-start.5) | collective-permute-done | bytes 32800 | tf_op jit(solution)/shard_map/ppermute | solution.py:19
  77.5 1.3 collective-permute-start.6
  78.8 4.5 %collective-permute-start.7 = (f32[4,16,1,256]{3,1,2,0:T(8,128)S(1)}, f32[4,16,1,256]{3,1,2,0:T(8,128)S(1)}, u32[]{:S(2)}, u32[]{:S(2)}) collective-permute-start(f32[4,16,1,256]{3,1,2,0:T(8,128)S(1)} %get-tuple-element.21), channel_id=1, source_target_pairs={{0,1},{1,2},{2,3},{4,5},{5,6},{6,7},{8,9},{9,10},{10,11},{12,13},{... | collective-permute-start | bytes 196616 | tf_op jit(solution)/shard_map/ppermute | solution.py:16
  83.6 1.6 %collective-permute-done.7 = f32[4,16,1,256]{3,1,2,0:T(8,128)S(1)} collective-permute-done((f32[4,16,1,256]{3,1,2,0:T(8,128)S(1)}, f32[4,16,1,256]{3,1,2,0:T(8,128)S(1)}, u32[]{:S(2)}, u32[]{:S(2)}) %collective-permute-start.7) | collective-permute-done | bytes 65568 | tf_op jit(solution)/shard_map/ppermute | solution.py:16
  85.5 4.3 %collective-permute-start.8 = (f32[4,16,1,256]{3,1,2,0:T(8,128)S(1)}, f32[4,16,1,256]{3,1,2,0:T(8,128)S(1)}, u32[]{:S(2)}, u32[]{:S(2)}) collective-permute-start(f32[4,16,1,256]{3,1,2,0:T(8,128)S(1)} %slice.248), channel_id=1, source_target_pairs={{0,1},{1,2},{2,3},{4,5},{5,6},{6,7},{8,9},{9,10},{10,11},{12,13},{... | collective-permute-start | bytes 196616 | tf_op jit(solution)/shard_map/ppermute | solution.py:27
  91.7 4.3 %collective-permute-done.9 = f32[4,16,1,256]{3,1,2,0:T(8,128)S(1)} collective-permute-done((f32[4,16,1,256]{3,1,2,0:T(8,128)S(1)}, f32[4,16,1,256]{3,1,2,0:T(8,128)S(1)}, u32[]{:S(2)}, u32[]{:S(2)}) %collective-permute-start.9) | collective-permute-done | bytes 65568 | tf_op jit(solution)/shard_map/ppermute | solution.py:27
  96.2 3.4 %collective-permute-start.10 = (f32[4,16,1,256]{3,1,2,0:T(8,128)S(1)}, f32[4,16,1,256]{3,1,2,0:T(8,128)S(1)}, u32[]{:S(2)}, u32[]{:S(2)}) collective-permute-start(f32[4,16,1,256]{3,1,2,0:T(8,128)S(1)} %get-tuple-element.15), channel_id=1, source_target_pairs={{0,1},{1,2},{2,3},{4,5},{5,6},{6,7},{8,9},{9,10},{10,11},{12,13},{... | collective-permute-start | bytes 196616 | tf_op jit(solution)/shard_map/ppermute | solution.py:16
  99.6 1.3 collective-permute-start.11
  101.5 4.3 %collective-permute-done.11 = f32[4,16,1,256]{3,1,2,0:T(8,128)S(1)} collective-permute-done((f32[4,16,1,256]{3,1,2,0:T(8,128)S(1)}, f32[4,16,1,256]{3,1,2,0:T(8,128)S(1)}, u32[]{:S(2)}, u32[]{:S(2)}) %collective-permute-start.11) | collective-permute-done | bytes 65568 | tf_op jit(solution)/shard_map/ppermute | solution.py:19
  106.0 2.5 %slice.224 = f32[4,16,2,128]{3,1,2,0:T(8,128)S(1)} slice(f32[4,16,2,258]{3,1,2,0:T(8,128)S(1)} %pad.37), slice={[0:4:1], [0:16:1], [0:2:1], [0:256:2]} | slice | bytes 131072 | tf_op jit(solution)/shard_map/slice | solution.py:63
  108.5 2.5 %slice.225 = f32[4,16,2,128]{3,1,2,0:T(8,128)S(1)} slice(f32[4,16,2,258]{3,1,2,0:T(8,128)S(1)} %pad.37), slice={[0:4:1], [0:16:1], [0:2:1], [3:258:2]} | slice | bytes 131072 | tf_op jit(solution)/shard_map/slice | solution.py:63
  111.0 2.5 %slice.222 = f32[4,16,2,128]{3,1,2,0:T(8,128)S(1)} slice(f32[4,16,2,256]{3,1,2,0:T(8,128)S(1)} %multiply_add_fusion), slice={[0:4:1], [0:16:1], [0:2:1], [0:256:2]} | slice | bytes 131072 | tf_op jit(solution)/shard_map/slice | solution.py:62
  113.5 2.5 %slice.223 = f32[4,16,2,128]{3,1,2,0:T(8,128)S(1)} slice(f32[4,16,2,256]{3,1,2,0:T(8,128)S(1)} %multiply_add_fusion), slice={[0:4:1], [0:16:1], [0:2:1], [1:256:2]} | slice | bytes 131072 | tf_op jit(solution)/shard_map/slice | solution.py:62
  116.0 9.8 %all_gather.3 = f32[4,128,2,128]{3,1,2,0:T(8,128)S(1)} all-gather(f32[4,16,2,128]{3,1,2,0:T(8,128)S(1)} %multiply_add_fusion.1), channel_id=1, replica_groups=mesh['mem'=8,'grid'=4] {'mem'}, dimensions={1}, use_global_device_ids=true | all-gather | bytes 589824 | tf_op jit(solution)/shard_map/all_gather | solution.py:116
  127.5 4.6 %collective-permute-start.13 = (f32[2,128,1,128]{1,3,2,0:T(8,128)S(1)}, f32[2,128,1,128]{1,3,2,0:T(8,128)S(1)}, u32[]{:S(2)}, u32[]{:S(2)}) collective-permute-start(f32[2,128,1,128]{1,3,2,0:T(8,128)S(1)} %get-tuple-element.14), channel_id=1, source_target_pairs={{0,1},{1,2},{2,3},{4,5},{5,6},{6,7},{8,9},{9,10},{10,11},{12,13},{... | collective-permute-start | bytes 393224 | tf_op jit(solution)/shard_map/ppermute | solution.py:16
  132.1 1.8 %collective-permute-done.12 = f32[2,128,1,128]{1,3,2,0:T(8,128)S(1)} collective-permute-done((f32[2,128,1,128]{1,3,2,0:T(8,128)S(1)}, f32[2,128,1,128]{1,3,2,0:T(8,128)S(1)}, u32[]{:S(2)}, u32[]{:S(2)}) %collective-permute-start.12) | collective-permute-done | bytes 131104 | tf_op jit(solution)/shard_map/ppermute | solution.py:19
  136.4 5.0 %collective-permute-start.15 = (f32[2,128,1,128]{1,3,2,0:T(8,128)S(1)}, f32[2,128,1,128]{1,3,2,0:T(8,128)S(1)}, u32[]{:S(2)}, u32[]{:S(2)}) collective-permute-start(f32[2,128,1,128]{1,3,2,0:T(8,128)S(1)} %get-tuple-element.12), channel_id=1, source_target_pairs={{0,1},{1,2},{2,3},{4,5},{5,6},{6,7},{8,9},{9,10},{10,11},{12,13},{... | collective-permute-start | bytes 393224 | tf_op jit(solution)/shard_map/ppermute | solution.py:16
  142.5 1.5 collective-permute-done.15
  (70 shorter events, 22.2 us)
Async XLA Ops:
  6.5 1.1 copy-start
  6.5 17.4 %copy-start.1 = (bf16[2,4,128,2,128]{4,3,2,1,0:T(2,128)(2,1)S(1)}, bf16[2,4,128,2,128]{4,3,2,1,0:T(2,128)(2,1)}, u32[]{:S(2)}) copy-start(bf16[2,4,128,2,128]{4,3,2,1,0:T(2,128)(2,1)} %param.6) | copy-start | bytes 1572868
  6.5 58.2 %reduce-scatter.2.cloned.1.call-start = ((), (), s32[]{:S(2)}) async-start(), calls=%async_computation.1 | async-start | bytes 589824 | tf_op jit(solution)/shard_map/reduce_scatter | solution.py:106
  7.9 8.4 %collective-permute-start = (f32[2,128,1,128]{1,3,2,0:T(8,128)S(1)}, f32[2,128,1,128]{1,3,2,0:T(8,128)S(1)}, u32[]{:S(2)}, u32[]{:S(2)}) collective-permute-start(f32[2,128,1,128]{1,3,2,0:T(8,128)S(1)} %get-tuple-element.26), channel_id=1, source_target_pairs={{1,0},{2,1},{3,2},{5,4},{6,5},{7,6},{9,8},{10,9},{11,10},{13,12},{... | collective-permute-start | bytes 393224 | tf_op jit(solution)/shard_map/ppermute | solution.py:19
  9.2 8.3 %collective-permute-start.1 = (f32[2,128,1,128]{1,3,2,0:T(8,128)S(1)}, f32[2,128,1,128]{1,3,2,0:T(8,128)S(1)}, u32[]{:S(2)}, u32[]{:S(2)}) collective-permute-start(f32[2,128,1,128]{1,3,2,0:T(8,128)S(1)} %get-tuple-element.27), channel_id=1, source_target_pairs={{0,1},{1,2},{2,3},{4,5},{5,6},{6,7},{8,9},{9,10},{10,11},{12,13},{... | collective-permute-start | bytes 393224 | tf_op jit(solution)/shard_map/ppermute | solution.py:16
  17.6 7.3 %collective-permute-start.2 = (f32[2,128,1,128]{1,3,2,0:T(8,128)S(1)}, f32[2,128,1,128]{1,3,2,0:T(8,128)S(1)}, u32[]{:S(2)}, u32[]{:S(2)}) collective-permute-start(f32[2,128,1,128]{1,3,2,0:T(8,128)S(1)} %get-tuple-element.24), channel_id=1, source_target_pairs={{1,0},{2,1},{3,2},{5,4},{6,5},{7,6},{9,8},{10,9},{11,10},{13,12},{... | collective-permute-start | bytes 393224 | tf_op jit(solution)/shard_map/ppermute | solution.py:19
  18.9 7.5 %collective-permute-start.3 = (f32[2,128,1,128]{1,3,2,0:T(8,128)S(1)}, f32[2,128,1,128]{1,3,2,0:T(8,128)S(1)}, u32[]{:S(2)}, u32[]{:S(2)}) collective-permute-start(f32[2,128,1,128]{1,3,2,0:T(8,128)S(1)} %get-tuple-element.25), channel_id=1, source_target_pairs={{0,1},{1,2},{2,3},{4,5},{5,6},{6,7},{8,9},{9,10},{10,11},{12,13},{... | collective-permute-start | bytes 393224 | tf_op jit(solution)/shard_map/ppermute | solution.py:16
  24.3 45.9 %copy-start.2 = (s32[4,256]{1,0:T(4,128)S(1)}, s32[4,256]{1,0:T(4,128)}, u32[]{:S(2)}) copy-start(s32[4,256]{1,0:T(4,128)} %param.10) | copy-start | bytes 12292
  24.3 45.9 %copy-start.3 = (s32[4,256]{1,0:T(4,128)S(1)}, s32[4,256]{1,0:T(4,128)}, u32[]{:S(2)}) copy-start(s32[4,256]{1,0:T(4,128)} %param.11) | copy-start | bytes 12292
  65.5 5.0 %collective-permute-start.4 = (f32[4,16,1,128]{3,1,2,0:T(8,128)S(1)}, f32[4,16,1,128]{3,1,2,0:T(8,128)S(1)}, u32[]{:S(2)}, u32[]{:S(2)}) collective-permute-start(f32[4,16,1,128]{3,1,2,0:T(8,128)S(1)} %get-tuple-element.32), channel_id=1, source_target_pairs={{0,1},{1,2},{2,3},{4,5},{5,6},{6,7},{8,9},{9,10},{10,11},{12,13},{... | collective-permute-start | bytes 98312 | tf_op jit(solution)/shard_map/ppermute | solution.py:16
  68.9 5.8 %collective-permute-start.5 = (f32[4,16,1,128]{3,1,2,0:T(8,128)S(1)}, f32[4,16,1,128]{3,1,2,0:T(8,128)S(1)}, u32[]{:S(2)}, u32[]{:S(2)}) collective-permute-start(f32[4,16,1,128]{3,1,2,0:T(8,128)S(1)} %get-tuple-element.33), channel_id=1, source_target_pairs={{1,0},{2,1},{3,2},{5,4},{6,5},{7,6},{9,8},{10,9},{11,10},{13,12},{... | collective-permute-start | bytes 98312 | tf_op jit(solution)/shard_map/ppermute | solution.py:19
  75.8 7.6 %copy-start.4 = (f32[4,128]{1,0:T(4,128)S(1)}, f32[4,128]{1,0:T(4,128)}, u32[]{:S(2)}) copy-start(f32[4,128]{1,0:T(4,128)} %param.9) | copy-start | bytes 6148
  77.5 6.2 %collective-permute-start.6 = (f32[4,16,1,256]{3,1,2,0:T(8,128)S(1)}, f32[4,16,1,256]{3,1,2,0:T(8,128)S(1)}, u32[]{:S(2)}, u32[]{:S(2)}) collective-permute-start(f32[4,16,1,256]{3,1,2,0:T(8,128)S(1)} %get-tuple-element.20), channel_id=1, source_target_pairs={{1,0},{2,1},{3,2},{5,4},{6,5},{7,6},{9,8},{10,9},{11,10},{13,12},{... | collective-permute-start | bytes 196616 | tf_op jit(solution)/shard_map/ppermute | solution.py:19
  78.8 6.4 %collective-permute-start.7 = (f32[4,16,1,256]{3,1,2,0:T(8,128)S(1)}, f32[4,16,1,256]{3,1,2,0:T(8,128)S(1)}, u32[]{:S(2)}, u32[]{:S(2)}) collective-permute-start(f32[4,16,1,256]{3,1,2,0:T(8,128)S(1)} %get-tuple-element.21), channel_id=1, source_target_pairs={{0,1},{1,2},{2,3},{4,5},{5,6},{6,7},{8,9},{9,10},{10,11},{12,13},{... | collective-permute-start | bytes 196616 | tf_op jit(solution)/shard_map/ppermute | solution.py:16
  85.5 6.2 %collective-permute-start.8 = (f32[4,16,1,256]{3,1,2,0:T(8,128)S(1)}, f32[4,16,1,256]{3,1,2,0:T(8,128)S(1)}, u32[]{:S(2)}, u32[]{:S(2)}) collective-permute-start(f32[4,16,1,256]{3,1,2,0:T(8,128)S(1)} %slice.248), channel_id=1, source_target_pairs={{0,1},{1,2},{2,3},{4,5},{5,6},{6,7},{8,9},{9,10},{10,11},{12,13},{... | collective-permute-start | bytes 196616 | tf_op jit(solution)/shard_map/ppermute | solution.py:27
  89.8 6.2 %collective-permute-start.9 = (f32[4,16,1,256]{3,1,2,0:T(8,128)S(1)}, f32[4,16,1,256]{3,1,2,0:T(8,128)S(1)}, u32[]{:S(2)}, u32[]{:S(2)}) collective-permute-start(f32[4,16,1,256]{3,1,2,0:T(8,128)S(1)} %slice.251), channel_id=1, source_target_pairs={{1,0},{2,1},{3,2},{5,4},{6,5},{7,6},{9,8},{10,9},{11,10},{13,12},{... | collective-permute-start | bytes 196616 | tf_op jit(solution)/shard_map/ppermute | solution.py:27
  96.2 5.3 %collective-permute-start.10 = (f32[4,16,1,256]{3,1,2,0:T(8,128)S(1)}, f32[4,16,1,256]{3,1,2,0:T(8,128)S(1)}, u32[]{:S(2)}, u32[]{:S(2)}) collective-permute-start(f32[4,16,1,256]{3,1,2,0:T(8,128)S(1)} %get-tuple-element.15), channel_id=1, source_target_pairs={{0,1},{1,2},{2,3},{4,5},{5,6},{6,7},{8,9},{9,10},{10,11},{12,13},{... | collective-permute-start | bytes 196616 | tf_op jit(solution)/shard_map/ppermute | solution.py:16
  99.6 6.2 %collective-permute-start.11 = (f32[4,16,1,256]{3,1,2,0:T(8,128)S(1)}, f32[4,16,1,256]{3,1,2,0:T(8,128)S(1)}, u32[]{:S(2)}, u32[]{:S(2)}) collective-permute-start(f32[4,16,1,256]{3,1,2,0:T(8,128)S(1)} %get-tuple-element.16), channel_id=1, source_target_pairs={{1,0},{2,1},{3,2},{5,4},{6,5},{7,6},{9,8},{10,9},{11,10},{13,12},{... | collective-permute-start | bytes 196616 | tf_op jit(solution)/shard_map/ppermute | solution.py:19
  126.2 7.7 %collective-permute-start.12 = (f32[2,128,1,128]{1,3,2,0:T(8,128)S(1)}, f32[2,128,1,128]{1,3,2,0:T(8,128)S(1)}, u32[]{:S(2)}, u32[]{:S(2)}) collective-permute-start(f32[2,128,1,128]{1,3,2,0:T(8,128)S(1)} %get-tuple-element.13), channel_id=1, source_target_pairs={{1,0},{2,1},{3,2},{5,4},{6,5},{7,6},{9,8},{10,9},{11,10},{13,12},{... | collective-permute-start | bytes 393224 | tf_op jit(solution)/shard_map/ppermute | solution.py:19
  127.5 7.5 %collective-permute-start.13 = (f32[2,128,1,128]{1,3,2,0:T(8,128)S(1)}, f32[2,128,1,128]{1,3,2,0:T(8,128)S(1)}, u32[]{:S(2)}, u32[]{:S(2)}) collective-permute-start(f32[2,128,1,128]{1,3,2,0:T(8,128)S(1)} %get-tuple-element.14), channel_id=1, source_target_pairs={{0,1},{1,2},{2,3},{4,5},{5,6},{6,7},{8,9},{9,10},{10,11},{12,13},{... | collective-permute-start | bytes 393224 | tf_op jit(solution)/shard_map/ppermute | solution.py:16
  135.1 7.3 %collective-permute-start.14 = (f32[2,128,1,128]{1,3,2,0:T(8,128)S(1)}, f32[2,128,1,128]{1,3,2,0:T(8,128)S(1)}, u32[]{:S(2)}, u32[]{:S(2)}) collective-permute-start(f32[2,128,1,128]{1,3,2,0:T(8,128)S(1)} %get-tuple-element.11), channel_id=1, source_target_pairs={{1,0},{2,1},{3,2},{5,4},{6,5},{7,6},{9,8},{10,9},{11,10},{13,12},{... | collective-permute-start | bytes 393224 | tf_op jit(solution)/shard_map/ppermute | solution.py:19
  136.4 7.5 %collective-permute-start.15 = (f32[2,128,1,128]{1,3,2,0:T(8,128)S(1)}, f32[2,128,1,128]{1,3,2,0:T(8,128)S(1)}, u32[]{:S(2)}, u32[]{:S(2)}) collective-permute-start(f32[2,128,1,128]{1,3,2,0:T(8,128)S(1)} %get-tuple-element.12), channel_id=1, source_target_pairs={{0,1},{1,2},{2,3},{4,5},{5,6},{6,7},{8,9},{9,10},{10,11},{12,13},{... | collective-permute-start | bytes 393224 | tf_op jit(solution)/shard_map/ppermute | solution.py:16
Sparse Core Ops, SparseCore 0:
  27.8 36.8 reduce-scatter.1
where the time goes:
time: 153 us; the launch traced here: 152 us
  waiting for transfers between devices  63.2 us (41%)
  starting transfers between devices  46.1 us (30%)
  local copies, waits for them, and re-layouts  15.4 us (10%)
  between operations  13.9 us (9%)
  blocking collectives  9.8 us (6%)
  other arithmetic  3.04 us (2%)
    reduce_scatter x1, waiting for transfers between devices, per_device(): lax.psum_scatter(partial_value, 'mem', scatter_dimension=1, tiled=True)  37 us
    ppermute x7, starting transfers between devices, with_halo(): lax.ppermute(lax.slice_in_dim(block, block.shape[dim] - width, None, axis...  31.5 us
    ppermute x7, waiting for transfers between devices, with_halo(): lax.ppermute(lax.slice_in_dim(block, 0, width, axis=dim), axis, backward)  13.6 us
    all_gather x1, blocking collectives, per_device(): lax.all_gather(coarsen(adjoint_fine, margin(adjoint_fine)), 'mem', axis=1...  9.8 us
    ppermute x7, starting transfers between devices, with_halo(): lax.ppermute(lax.slice_in_dim(block, 0, width, axis=dim), axis, backward)  9.04 us
    ppermute x7, waiting for transfers between devices, with_halo(): lax.ppermute(lax.slice_in_dim(block, block.shape[dim] - width, None, axis...  7.75 us
    ppermute x2, starting transfers between devices, shifted(): return lax.ppermute(shard, axis, pairs)  5.56 us
    slice x2, local copies, waits for them, and re-layouts, coarsen(): result = near_weight * (rows_coarse[..., 0::2] + rows_coarse[..., 1::2])  4.97 us
  transfers between devices with their start and end apart: 17, of which 17 were waited for; matrix products, arithmetic and copies ran while one was open for 0% of the time, Pallas kernels for 0%

commit v1 on v0

v1 whole, which is shorter than its diff:
```python
import functools
import jax
import jax.numpy as jnp
from jax import lax
from jax.experimental import pallas as pl
from jax.experimental.pallas import tpu as pltpu
from jax.sharding import PartitionSpec as P

diffusion = 0.2
near_weight = 0.75
far_weight = 0.25
f32 = jnp.float32
MESH = pl.DeviceIdType.MESH


def columns(x, by):
    width = x.shape[-1]
    lane = lax.broadcasted_iota(jnp.int32, x.shape, x.ndim - 1)
    moved = pltpu.roll(x, by % width, x.ndim - 1)
    edge = 0 if by == 1 else width - 1
    return jnp.where(lane == edge, 0.0, moved)


def smooth(prev, center, after):
    sides = columns(center, 1) + columns(center, -1)
    return center + diffusion * (after + prev + sides - 4.0 * center)


def smooth_twice(rows, low, high):
    first = [smooth(rows[i - 1], rows[i], rows[i + 1]) for i in range(1, len(rows) - 1)]
    first[0] = first[0] * low
    first[-1] = first[-1] * high
    return [smooth(first[i - 1], first[i], first[i + 1]) for i in range(1, len(first) - 1)]


def kernel(cfg, ens_hbm, ctl_ref, vert_ref, ivar_ref, code_ref, count_ref, out_ref,
           ens_ref, ensf, ctlf, ext, part, r1, half, r2, share, adj, proj, obs, rnd,
           ens_sem, a_s, a_r, b1_s, b1_r, b2_s, b2_r, c_s, c_r, d_s, d_r, p_s, p_r, e_s, e_r, o_s, o_r):
    KC, Q, M, G, R, KM, V, L, n, W, group = cfg
    NB = L // n
    HB = 2 * Q
    factor = (KM * M) ** (-0.5)
    mem = lax.axis_index("mem")
    grid = lax.axis_index("grid")
    core = lax.rem(mem, 2)
    chip = lax.div(mem, 2)
    partner = chip * 2 + (1 - core)
    has_prev = grid > 0
    has_next = grid < G - 1
    before = (mem, jnp.maximum(grid - 1, 0))
    behind = (mem, jnp.minimum(grid + 1, G - 1))
    low = jnp.where(has_prev, 1.0, 0.0).astype(f32)
    high = jnp.where(has_next, 1.0, 0.0).astype(f32)

    def peer(d):
        return (lax.rem(chip + d, Q) * 2 + core, grid)

    barrier = pltpu.get_barrier_semaphore()

    def greet(device):
        pl.semaphore_signal(barrier, inc=1, device_id=device, device_id_type=MESH)

    @pl.when(has_prev)
    def _():
        greet(before)

    @pl.when(has_next)
    def _():
        greet(behind)

    greet((partner, grid))
    for d in range(1, Q):
        greet(peer(d))

    ens_copy = pltpu.make_async_copy(ens_hbm, ens_ref, ens_sem)
    ens_copy.start()

    def up_copy(buf, lead, rows, s, r, at):
        return pltpu.make_async_remote_copy(
            src_ref=buf.at[lead + (pl.ds(rows, 2),)], dst_ref=buf.at[lead + (pl.ds(0, 2),)],
            send_sem=s.at[at, 0], recv_sem=r.at[at, 0], device_id=behind, device_id_type=MESH)

    def down_copy(buf, lead, rows, s, r, at):
        return pltpu.make_async_remote_copy(
            src_ref=buf.at[lead + (pl.ds(2, 2),)], dst_ref=buf.at[lead + (pl.ds(rows + 2, 2),)],
            send_sem=s.at[at, 1], recv_sem=r.at[at, 1], device_id=before, device_id_type=MESH)

    def halo_start(*args):
        @pl.when(has_next)
        def _():
            up_copy(*args).start()

        @pl.when(has_prev)
        def _():
            down_copy(*args).start()

    def halo_recv(*args):
        @pl.when(has_prev)
        def _():
            up_copy(*args).wait_recv()

        @pl.when(has_next)
        def _():
            down_copy(*args).wait_recv()

    def halo_sent(*args):
        @pl.when(has_next)
        def _():
            up_copy(*args).wait_send()

        @pl.when(has_prev)
        def _():
            down_copy(*args).wait_send()

    def a_args(j):
        return ext, (j,), R, a_s, a_r, j

    def c_args(j):
        return share, (j,), R, c_s, c_r, j

    def e_args(j):
        return proj, (j,), R, e_s, e_r, j

    o_args = (obs, (), 2 * R, o_s, o_r, 0)

    def core_copy(j):
        return pltpu.make_async_remote_copy(
            src_ref=part.at[j, 1 - core], dst_ref=r1.at[j], send_sem=b1_s.at[j], recv_sem=b1_r.at[j],
            device_id=(partner, grid), device_id_type=MESH)

    def chip_copy(j, d):
        return pltpu.make_async_remote_copy(
            src_ref=half.at[j, lax.rem(chip + d, Q)], dst_ref=r2.at[j, d],
            send_sem=b2_s.at[j, d], recv_sem=b2_r.at[j, d], device_id=peer(d), device_id_type=MESH)

    def gather_copy(j, d):
        return pltpu.make_async_remote_copy(
            src_ref=adj.at[j, core, chip], dst_ref=adj.at[j, core, chip],
            send_sem=d_s.at[j, d], recv_sem=d_r.at[j, d], device_id=peer(d), device_id_type=MESH)

    def pass_copy(j, d):
        source = lax.rem(chip + Q - d, Q)
        return pltpu.make_async_remote_copy(
            src_ref=adj.at[j, core, source], dst_ref=adj.at[j, core, source],
            send_sem=p_s.at[j, d], recv_sem=p_r.at[j, d], device_id=(partner, grid), device_id_type=MESH)

    ctlf[...] = ctl_ref[...].astype(f32)
    wide = jnp.concatenate(
        [ctlf[k, :, pl.ds(r, n, stride=R), :].reshape(L, W).astype(jnp.bfloat16)
         for k in range(KM) for r in range(R)], axis=1)
    mixed = jnp.dot(vert_ref[...], wide, preferred_element_type=f32)
    for k in range(KM):
        for r in range(R):
            at = (k * R + r) * W
            ext[:, 2 + r, k] = mixed[:, at:at + W].reshape(KC, HB, n, W)

    def pick():
        i = lax.broadcasted_iota(jnp.int32, (2 * W, 2 * W), 0)
        o = lax.broadcasted_iota(jnp.int32, (2 * W, 2 * W), 1)
        return jnp.where(i == 2 * lax.rem(o, W) + lax.div(o, W), 1.0, 0.0).astype(jnp.bfloat16)

    ints = jnp.concatenate([code_ref[...], count_ref[...]], axis=0).astype(f32).astype(jnp.bfloat16)
    apart = jnp.dot(ints, pick(), preferred_element_type=f32)
    for i in range(2 * R):
        for p in range(2):
            obs[2 + i, p:p + 1, :] = apart[i:i + 1, p * W:(p + 1) * W]
            obs[2 + i, 2 + p:3 + p, :] = apart[2 * R + i:2 * R + i + 1, p * W:(p + 1) * W]
        obs[2 + i, 4:8, :] = jnp.zeros((4, W), f32)

    @pl.when(jnp.logical_not(has_prev))
    def _():
        ext[:, 0:2] = jnp.zeros((KC, 2) + ext.shape[2:], f32)
        proj[:, 0:2] = jnp.zeros((KC, 2) + proj.shape[2:], f32)
        share[:, 0:2] = jnp.zeros((KC, 2) + share.shape[2:], f32)
        obs[0:2] = jnp.zeros((2,) + obs.shape[1:], f32)

    @pl.when(jnp.logical_not(has_next))
    def _():
        ext[:, R + 2:R + 4] = jnp.zeros((KC, 2) + ext.shape[2:], f32)
        proj[:, R + 2:R + 4] = jnp.zeros((KC, 2) + proj.shape[2:], f32)
        share[:, R + 2:R + 4] = jnp.zeros((KC, 2) + share.shape[2:], f32)
        obs[2 * R + 2:2 * R + 4] = jnp.zeros((2,) + obs.shape[1:], f32)

    pl.semaphore_wait(barrier, Q + has_prev.astype(jnp.int32) + has_next.astype(jnp.int32))

    for j in range(KC):
        halo_start(*a_args(j))
    halo_start(*o_args)

    ens_copy.wait()
    for k in range(KM):
        def widen(v, _):
            ensf[k, v] = ens_ref[k, v].astype(f32)
            return 0
        lax.fori_loop(0, V, widen, 0)

    halo_recv(*o_args)

    def member(k, v, b0, r):
        return ensf[k, v, pl.ds(b0, group), pl.ds(r, n, stride=R), :]

    for j in range(KC):
        halo_recv(*a_args(j))

        def weigh(g, _, j=j):
            b0 = g * group
            local = [smooth_twice([ext[j, i, k, pl.ds(b0, group)] for i in range(R + 4)], low, high)
                     for k in range(KM)]
            c, q0 = lax.div(b0, Q), lax.rem(b0, Q)
            for v in range(V):
                for r in range(R):
                    total = member(0, v, j * HB + b0, r) * local[0][r]
                    for k in range(1, KM):
                        total = total + member(k, v, j * HB + b0, r) * local[k][r]
                    part[j, c, pl.ds(q0, group), v, r] = factor * total
            return 0

        lax.fori_loop(0, HB // group, weigh, 0)
        core_copy(j).start()

    for j in range(KC):
        core_copy(j).wait_recv()

        def join(q, _, j=j):
            half[j, q] = part[j, core, q] + r1[j, q]
            return 0

        lax.fori_loop(0, Q, join, 0)
        for d in range(Q - 1, 0, -1):
            chip_copy(j, d).start()

    for j in range(KC):
        total = half[j, chip]
        for d in range(1, Q):
            chip_copy(j, d).wait_recv()
            total = total + r2[j, d]
        for r in range(R):
            share[j, 2 + r] = total[:, r]
        halo_start(*c_args(j))

    for j in range(KC):
        first_level = (j * HB + core * Q + chip) * n
        hot = (lax.broadcasted_iota(jnp.int32, (n, L), 1)
               == lax.broadcasted_iota(jnp.int32, (n, L), 0) + first_level)
        weights = jnp.stack(
            [jnp.broadcast_to(jnp.sum(jnp.where(hot, ivar_ref[v:v + 1, :], 0.0), axis=1, keepdims=True), (n, W))
             for v in range(V)], axis=0)
        halo_recv(*c_args(j))
        u = [share[j, i] for i in range(R + 4)]
        fine = []
        last = 2 * R + 3
        for i in range(last + 1):
            a = i // 2 + 1
            row = near_weight * u[a] + far_weight * (u[a - 1] if i % 2 == 0 else u[a + 1])
            if i < 2:
                row = row * low
            if i > last - 2:
                row = row * high
            fine.append((near_weight * row + far_weight * columns(row, 1),
                         near_weight * row + far_weight * columns(row, -1)))
        forced, ups, downs = [], [], []
        for i in range(last + 1):
            even_odd, up, down = [], [], []
            right_of = (fine[i][1], columns(fine[i][0], -1)) if 0 < i < last else None
            left_of = (columns(fine[i][1], 1), fine[i][0]) if 0 < i < last else None
            sides = []
            for p in range(2):
                code = obs[i, p:p + 1, :]
                scale = obs[i, 2 + p:3 + p, :] * weights
                m = [jnp.where(code == which, 1.0, 0.0) for which in range(1, 5)]
                diff = fine[i][p]
                if i < last:
                    diff = diff - m[0] * fine[i + 1][p]
                if i > 0:
                    diff = diff - m[1] * fine[i - 1][p]
                if right_of is not None:
                    diff = diff - m[2] * right_of[p] - m[3] * left_of[p]
                force = scale * diff
                even_odd.append(force)
                up.append(m[0] * force)
                down.append(m[1] * force)
                sides.append((m[2] * force, m[3] * force))
            ups.append(up)
            downs.append(down)
            if 0 < i < last:
                even = even_odd[0] - columns(sides[1][0], 1) - sides[1][1]
                odd = even_odd[1] - sides[0][0] - columns(sides[0][1], -1)
                forced.append((even, odd))
            else:
                forced.append(None)
        back = [None] * (last + 1)
        for i in range(1, last):
            pair = [forced[i][p] - ups[i - 1][p] - downs[i + 1][p] for p in range(2)]
            if i == 1:
                pair = [x * low for x in pair]
            if i == last - 1:
                pair = [x * high for x in pair]
            back[i] = pair
        for r in range(R):
            i = 2 * r + 2
            even, odd = [near_weight * (back[i][p] + back[i + 1][p]) + far_weight * (back[i - 1][p] + back[i + 2][p])
                         for p in range(2)]
            row = near_weight * (even + odd) + far_weight * (columns(odd, 1) + columns(even, -1))
            adj[j, core, chip, :, r] = row
        for d in range(Q - 1, 0, -1):
            gather_copy(j, d).start()
        pass_copy(j, 0).start()

    for j in range(KC):
        for d in range(1, Q):
            gather_copy(j, d).wait_recv()
            pass_copy(j, d).start()

    def arrived(j, d):
        source = lax.rem(chip + Q - d, Q)
        return pltpu.make_async_remote_copy(
            src_ref=adj.at[j, 1 - core, source], dst_ref=adj.at[j, 1 - core, source],
            send_sem=p_s.at[j, d], recv_sem=p_r.at[j, d], device_id=(partner, grid), device_id_type=MESH)

    for j in range(KC):
        for d in range(Q):
            arrived(j, d).wait_recv()

        def project(g, _, j=j):
            b0 = g * group
            c, q0 = lax.div(b0, Q), lax.rem(b0, Q)
            for r in range(R):
                fields = [adj[j, c, pl.ds(q0, group), v, r] for v in range(V)]
                for k in range(KM):
                    total = member(k, 0, j * HB + b0, r) * fields[0]
                    for v in range(1, V):
                        total = total + member(k, v, j * HB + b0, r) * fields[v]
                    proj[j, 2 + r, k, pl.ds(b0, group)] = factor * total
            return 0

        lax.fori_loop(0, HB // group, project, 0)
        halo_start(*e_args(j))

    for j in range(KC):
        halo_recv(*e_args(j))

        def settle(g, _, j=j):
            b0 = g * group
            for k in range(KM):
                rows = smooth_twice([proj[j, i, k, pl.ds(b0, group)] for i in range(R + 4)], low, high)
                for r in range(R):
                    rnd[k, r, pl.ds(j * HB + b0, group)] = rows[r]
            return 0

        lax.fori_loop(0, HB // group, settle, 0)

    wide = jnp.concatenate(
        [rnd[k, r].reshape(L, W).astype(jnp.bfloat16) for k in range(KM) for r in range(R)], axis=1)
    product = lax.dot_general(vert_ref[...], wide, (((0,), (0,)), ((), ())), preferred_element_type=f32)
    for k in range(KM):
        for r in range(R):
            at = (k * R + r) * W
            out_ref[k, :, pl.ds(r, n, stride=R), :] = (
                ctlf[k, :, pl.ds(r, n, stride=R), :] + product[:, at:at + W].reshape(NB, n, W))

    halo_sent(*o_args)
    for j in range(KC):
        halo_sent(*a_args(j))
        core_copy(j).wait_send()
        for d in range(1, Q):
            chip_copy(j, d).wait_send()
            gather_copy(j, d).wait_send()
        halo_sent(*c_args(j))
        for d in range(Q):
            pass_copy(j, d).wait_send()
        halo_sent(*e_args(j))


def per_device(ensemble, control, vertical, inverse_var, obs_code, obs_count):
    KM, V, L, R, W = ensemble.shape
    M = lax.axis_size("mem")
    G = lax.axis_size("grid")
    Q = M // 2
    levels = L // M
    KC = 2 if levels % 16 == 0 else 1
    n = levels // KC
    NB = L // n
    HB = 2 * Q
    group = 4 if Q % 4 == 0 else 1
    cfg = (KC, Q, M, G, R, KM, V, L, n, W, group)
    vmem = pl.BlockSpec(memory_space=pltpu.VMEM)
    dma = pltpu.SemaphoreType.DMA
    out = pl.pallas_call(
        functools.partial(kernel, cfg),
        out_shape=jax.ShapeDtypeStruct((KM, NB, n * R, W), f32),
        in_specs=[pl.BlockSpec(memory_space=pl.ANY)] + [vmem] * 5,
        out_specs=vmem,
        scratch_shapes=[
            pltpu.VMEM((KM, V, NB, n * R, W), jnp.bfloat16),
            pltpu.VMEM((KM, V, NB, n * R, W), f32),
            pltpu.VMEM((KM, NB, n * R, W), f32),
            pltpu.VMEM((KC, R + 4, KM, HB, n, W), f32),
            pltpu.VMEM((KC, 2, Q, V, R, n, W), f32),
            pltpu.VMEM((KC, Q, V, R, n, W), f32),
            pltpu.VMEM((KC, Q, V, R, n, W), f32),
            pltpu.VMEM((KC, Q, V, R, n, W), f32),
            pltpu.VMEM((KC, R + 4, V, n, W), f32),
            pltpu.VMEM((KC, 2, Q, V, R, n, W), f32),
            pltpu.VMEM((KC, R + 4, KM, HB, n, W), f32),
            pltpu.VMEM((2 * R + 4, 8, W), f32),
            pltpu.VMEM((KM, R, NB, n, W), f32),
            dma,
            dma((KC, 2)), dma((KC, 2)),
            dma((KC,)), dma((KC,)),
            dma((KC, Q)), dma((KC, Q)),
            dma((KC, 2)), dma((KC, 2)),
            dma((KC, Q)), dma((KC, Q)),
            dma((KC, Q)), dma((KC, Q)),
            dma((KC, 2)), dma((KC, 2)),
            dma((1, 2)), dma((1, 2)),
        ],
        compiler_params=pltpu.CompilerParams(collective_id=0, has_side_effects=True),
    )(
        ensemble.reshape(KM, V, NB, n * R, W),
        control.reshape(KM, NB, n * R, W),
        vertical,
        inverse_var,
        obs_code,
        obs_count,
    )
    return out.reshape(KM, L, R, W)


def solution(mesh):
    return jax.shard_map(
        per_device,
        mesh=mesh,
        in_specs=(
            P("mem", None, None, "grid", None),
            P("mem", None, "grid", None),
            P(),
            P(),
            P("grid", None),
            P("grid", None),
        ),
        out_specs=P("mem", None, "grid", None),
        check_vma=False,
    )
```

time: 153 us -> 38.6 us (0.25)
  waiting for transfers between devices: 63.2 us -> 0 us
  starting transfers between devices: 46.1 us -> 0 us
  Pallas kernels: 0 us -> 36.8 us
  between operations: 13.9 us -> 0.01 us
  local copies, waits for them, and re-layouts: 15.4 us -> 1.67 us
  blocking collectives: 9.8 us -> 0 us
  other arithmetic: 3.04 us -> 0 us
    ppermute x16 -> x0, starting transfers between devices: 46.1 us -> none  [the longest x7 31.5 us: with_halo(): lax.ppermute(lax.slice_in_dim(block, block.shape[dim] - width, None, axis...]
    reduce_scatter x1 -> x0, waiting for transfers between devices: 37 us -> none  [per_device(): lax.psum_scatter(partial_value, 'mem', scatter_dimension=1, tiled=True)]
    pallas_call x0 -> x1, Pallas kernels: none -> 36.8 us  [per_device(): pl.pallas_call(functools.partial(kernel, cfg), out_shape=jax.ShapeDtypeSt...]
    ppermute x16 -> x0, waiting for transfers between devices: 26.2 us -> none  [the longest x7 13.6 us: with_halo(): lax.ppermute(lax.slice_in_dim(block, 0, width, axis=dim), axis, backward)]
    slice x15 -> x0, local copies, waits for them, and re-layouts: 11.2 us -> none  [the longest x2 4.97 us: coarsen(): result = near_weight * (rows_coarse[..., 0::2] + rows_coarse[..., 1::2])]
    all_gather x1 -> x0, blocking collectives: 9.8 us -> none  [per_device(): lax.all_gather(coarsen(adjoint_fine, margin(adjoint_fine)), 'mem', axis=1...]
  transfers between devices with their start and end apart: 17 -> 0, of which waited for: 17 -> 0; matrix products, arithmetic and copies ran while one was open for 0% -> 0% of each run, Pallas kernels for 0% -> 0%
where the time goes in v1:
time: 38.6 us; the launch traced here: 38.4 us
  Pallas kernels  36.8 us (95%)
  local copies, waits for them, and re-layouts  1.67 us (4%)
    pallas_call x1, Pallas kernels, per_device(): pl.pallas_call(functools.partial(kernel, cfg), out_shape=jax.ShapeDtypeSt...  36.8 us
    unnamed x1, local copies, waits for them, and re-layouts  1.67 us

profile of v1, /device:TPU:0, one launch (start us, length us, event | category | flops | bytes accessed | tf_op | source)
XLA Modules:
  0.0 38.4 jit_solution(8781098197849264917)
XLA Ops:
  0.0 36.8 %shard_map.64 = f32[2,16,16,128]{3,2,1,0:T(8,128)} custom-call(bf16[2,4,16,16,128]{4,3,2,1,0:T(8,128)(2,1)} %bitcast.4, bf16[2,16,16,128]{3,2,1,0:T(8,128)(2,1)} %bitcast.5, bf16[128,128]{1,0:T(8,128)(2,1)} %vert_ref.1, f32[4,128]{1,0:T(4,128)} %ivar_ref.1, s32[4,256]{1,0:T(4,128)} %code_ref.1, s32[4,256]{1,0:T(4,128)} %count_ref.1), custom_call_target="tpu_custom_call" | custom-call | tf_op jit(solution)/shard_map/pallas_call | solution.py:388
  36.8 1.7 %copy.8 = f32[2,128,2,128]{3,2,1,0:T(2,128)} copy(f32[2,128,2,128]{3,2,1,0:T(2,128)} %bitcast.3) | data formatting | bytes 524288

commit v2 on v1

--- a/solution.py
+++ b/solution.py
@@ -31,6 +31,15 @@
     first[0] = first[0] * low
     first[-1] = first[-1] * high
     return [smooth(first[i - 1], first[i], first[i + 1]) for i in range(1, len(first) - 1)]
+
+
+LAG = (0, 15, 45, 70, 95, 105, 150)
+
+
+def order_of(chunks, count):
+    delay = 28
+    at = [(LAG[i] + delay * j, j, i) for j in range(chunks) for i in range(count)]
+    return [(i, j) for _, j, i in sorted(at)]
 
 
 def kernel(cfg, ens_hbm, ctl_ref, vert_ref, ivar_ref, code_ref, count_ref, out_ref,
@@ -199,10 +208,10 @@
     def member(k, v, b0, r):
         return ensf[k, v, pl.ds(b0, group), pl.ds(r, n, stride=R), :]
 
-    for j in range(KC):
+    def stage_weigh(j):
         halo_recv(*a_args(j))
 
-        def weigh(g, _, j=j):
+        def weigh(g, _):
             b0 = g * group
             local = [smooth_twice([ext[j, i, k, pl.ds(b0, group)] for i in range(R + 4)], low, high)
                      for k in range(KM)]
@@ -218,10 +227,10 @@
         lax.fori_loop(0, HB // group, weigh, 0)
         core_copy(j).start()
 
-    for j in range(KC):
+    def stage_join(j):
         core_copy(j).wait_recv()
 
-        def join(q, _, j=j):
+        def join(q, _):
             half[j, q] = part[j, core, q] + r1[j, q]
             return 0
 
@@ -229,7 +238,7 @@
         for d in range(Q - 1, 0, -1):
             chip_copy(j, d).start()
 
-    for j in range(KC):
+    def stage_reduce(j):
         total = half[j, chip]
         for d in range(1, Q):
             chip_copy(j, d).wait_recv()
@@ -238,7 +247,7 @@
             share[j, 2 + r] = total[:, r]
         halo_start(*c_args(j))
 
-    for j in range(KC):
+    def stage_observe(j):
         first_level = (j * HB + core * Q + chip) * n
         hot = (lax.broadcasted_iota(jnp.int32, (n, L), 1)
                == lax.broadcasted_iota(jnp.int32, (n, L), 0) + first_level)
@@ -306,7 +315,7 @@
             gather_copy(j, d).start()
         pass_copy(j, 0).start()
 
-    for j in range(KC):
+    def stage_forward(j):
         for d in range(1, Q):
             gather_copy(j, d).wait_recv()
             pass_copy(j, d).start()
@@ -317,11 +326,11 @@
             src_ref=adj.at[j, 1 - core, source], dst_ref=adj.at[j, 1 - core, source],
             send_sem=p_s.at[j, d], recv_sem=p_r.at[j, d], device_id=(partner, grid), device_id_type=MESH)
 
-    for j in range(KC):
+    def stage_project(j):
         for d in range(Q):
             arrived(j, d).wait_recv()
 
-        def project(g, _, j=j):
+        def project(g, _):
             b0 = g * group
             c, q0 = lax.div(b0, Q), lax.rem(b0, Q)
             for r in range(R):
@@ -336,10 +345,10 @@
         lax.fori_loop(0, HB // group, project, 0)
         halo_start(*e_args(j))
 
-    for j in range(KC):
+    def stage_settle(j):
         halo_recv(*e_args(j))
 
-        def settle(g, _, j=j):
+        def settle(g, _):
             b0 = g * group
             for k in range(KM):
                 rows = smooth_twice([proj[j, i, k, pl.ds(b0, group)] for i in range(R + 4)], low, high)
@@ -349,14 +358,17 @@
 
         lax.fori_loop(0, HB // group, settle, 0)
 
+    stages = (stage_weigh, stage_join, stage_reduce, stage_observe, stage_forward, stage_project, stage_settle)
+    for index, j in order_of(KC, len(stages)):
+        stages[index](j)
+
     wide = jnp.concatenate(
         [rnd[k, r].reshape(L, W).astype(jnp.bfloat16) for k in range(KM) for r in range(R)], axis=1)
     product = lax.dot_general(vert_ref[...], wide, (((0,), (0,)), ((), ())), preferred_element_type=f32)
     for k in range(KM):
         for r in range(R):
             at = (k * R + r) * W
-            out_ref[k, :, pl.ds(r, n, stride=R), :] = (
-                ctlf[k, :, pl.ds(r, n, stride=R), :] + product[:, at:at + W].reshape(NB, n, W))
+            out_ref[k, :, pl.ds(r, n, stride=R), :] = product[:, at:at + W].reshape(NB, n, W)
 
     halo_sent(*o_args)
     for j in range(KC):
@@ -385,7 +397,8 @@
     cfg = (KC, Q, M, G, R, KM, V, L, n, W, group)
     vmem = pl.BlockSpec(memory_space=pltpu.VMEM)
     dma = pltpu.SemaphoreType.DMA
-    out = pl.pallas_call(
+    member_control = control.reshape(KM, NB, n * R, W)
+    back = pl.pallas_call(
         functools.partial(kernel, cfg),
         out_shape=jax.ShapeDtypeStruct((KM, NB, n * R, W), f32),
         in_specs=[pl.BlockSpec(memory_space=pl.ANY)] + [vmem] * 5,
@@ -417,13 +430,13 @@
         compiler_params=pltpu.CompilerParams(collective_id=0, has_side_effects=True),
     )(
         ensemble.reshape(KM, V, NB, n * R, W),
-        control.reshape(KM, NB, n * R, W),
+        member_control,
         vertical,
         inverse_var,
         obs_code,
         obs_count,
     )
-    return out.reshape(KM, L, R, W)
+    return (member_control.astype(f32) + back).reshape(KM, L, R, W)
 
 
 def solution(mesh):

time: 38.6 us -> 37.5 us (0.972)
  other arithmetic: 0 us -> 1.68 us
  local copies, waits for them, and re-layouts: 1.67 us -> 0.01 us
  Pallas kernels: 36.8 us -> 35.7 us
    add x0 -> x1, other arithmetic: none -> 1.68 us  [per_device(): return (member_control.astype(f32) + back).reshape(KM, L, R, W)]
    unnamed x1 -> x2, local copies, waits for them, and re-layouts: 1.67 us -> 0.01 us
    pallas_call x1, Pallas kernels: 36.8 us -> 35.7 us  [per_device(): pl.pallas_call(functools.partial(kernel, cfg), out_shape=jax.ShapeDtypeSt...]
where the time goes in v2:
time: 37.5 us; the launch traced here: 37.4 us
  Pallas kernels  35.7 us (95%)
  other arithmetic  1.68 us (4%)
    pallas_call x1, Pallas kernels, per_device(): pl.pallas_call(functools.partial(kernel, cfg), out_shape=jax.ShapeDtypeSt...  35.7 us
    add x1, other arithmetic, per_device(): return (member_control.astype(f32) + back).reshape(KM, L, R, W)  1.68 us

profile of v2, /device:TPU:0, one launch (start us, length us, event | category | flops | bytes accessed | tf_op | source)
XLA Modules:
  0.0 37.4 jit_solution(16285269660895986590)
XLA Ops:
  0.0 0.0 copy-start
  0.0 35.7 %shard_map.64 = f32[2,16,16,128]{3,2,1,0:T(8,128)} custom-call(bf16[2,4,16,16,128]{4,3,2,1,0:T(8,128)(2,1)} %bitcast.5, bf16[2,16,16,128]{3,2,1,0:T(8,128)(2,1)} %bitcast.6, bf16[128,128]{1,0:T(8,128)(2,1)} %vert_ref.1, f32[4,128]{1,0:T(4,128)} %ivar_ref.1, s32[4,256]{1,0:T(4,128)} %code_ref.1, s32[4,256]{1,0:T(4,128)} %count_ref.1), custom_call_target="tpu_custom_call" | custom-call | tf_op jit(solution)/shard_map/pallas_call | solution.py:401
  35.7 0.0 copy-done
  35.7 1.7 %convert_add_fusion = f32[2,16,16,128]{3,2,1,0:T(8,128)} fusion(f32[2,16,16,128]{3,2,1,0:T(8,128)} %shard_map.64, bf16[2,16,16,128]{3,2,1,0:T(8,128)(2,1)S(1)} %bitcast.7), kind=kLoop, calls=%fused_computation | loop fusion | flops 131072 | bytes 655360 | tf_op jit(solution)/shard_map/add | solution.py:439
Async XLA Ops:
  0.0 35.7 %copy-start = (bf16[2,128,2,128]{3,2,1,0:T(2,128)(2,1)S(1)}, bf16[2,128,2,128]{3,2,1,0:T(2,128)(2,1)}, u32[]{:S(2)}) copy-start(bf16[2,128,2,128]{3,2,1,0:T(2,128)(2,1)} %param.7) | copy-start | bytes 393220

commit v3 on v2

--- a/solution.py
+++ b/solution.py
@@ -33,18 +33,18 @@
     return [smooth(first[i - 1], first[i], first[i + 1]) for i in range(1, len(first) - 1)]
 
 
-LAG = (0, 15, 45, 70, 95, 105, 150)
+LAG = (0, 20, 60, 90, 130, 140, 190)
 
 
 def order_of(chunks, count):
-    delay = 28
+    delay = 35
     at = [(LAG[i] + delay * j, j, i) for j in range(chunks) for i in range(count)]
     return [(i, j) for _, j, i in sorted(at)]
 
 
-def kernel(cfg, ens_hbm, ctl_ref, vert_ref, ivar_ref, code_ref, count_ref, out_ref,
-           ens_ref, ensf, ctlf, ext, part, r1, half, r2, share, adj, proj, obs, rnd,
-           ens_sem, a_s, a_r, b1_s, b1_r, b2_s, b2_r, c_s, c_r, d_s, d_r, p_s, p_r, e_s, e_r, o_s, o_r):
+def kernel(cfg, ens_hbm, ctl_hbm, vert_hbm, ivar_hbm, code_hbm, count_hbm, out_ref,
+           ens_ref, ctl_ref, vert_ref, ivar_ref, code_ref, count_ref, ensf, ctlf, ext, part, r1, half, r2, share, adj, proj, obs, rnd,
+           in_sem, a_s, a_r, b1_s, b1_r, b2_s, b2_r, c_s, c_r, d_s, d_r, p_s, p_r, e_s, e_r, o_s, o_r):
     KC, Q, M, G, R, KM, V, L, n, W, group = cfg
     NB = L // n
     HB = 2 * Q
@@ -81,8 +81,11 @@
     for d in range(1, Q):
         greet(peer(d))
 
-    ens_copy = pltpu.make_async_copy(ens_hbm, ens_ref, ens_sem)
-    ens_copy.start()
+    loads = [pltpu.make_async_copy(source, target, in_sem.at[i]) for i, (source, target) in enumerate((
+        (ctl_hbm, ctl_ref), (vert_hbm, vert_ref), (code_hbm, code_ref), (count_hbm, count_ref),
+        (ivar_hbm, ivar_ref), (ens_hbm, ens_ref)))]
+    for load in loads:
+        load.start()
 
     def up_copy(buf, lead, rows, s, r, at):
         return pltpu.make_async_remote_copy(
@@ -153,6 +156,8 @@
             src_ref=adj.at[j, core, source], dst_ref=adj.at[j, core, source],
             send_sem=p_s.at[j, d], recv_sem=p_r.at[j, d], device_id=(partner, grid), device_id_type=MESH)
 
+    loads[0].wait()
+    loads[1].wait()
     ctlf[...] = ctl_ref[...].astype(f32)
     wide = jnp.concatenate(
         [ctlf[k, :, pl.ds(r, n, stride=R), :].reshape(L, W).astype(jnp.bfloat16)
@@ -168,6 +173,8 @@
         o = lax.broadcasted_iota(jnp.int32, (2 * W, 2 * W), 1)
         return jnp.where(i == 2 * lax.rem(o, W) + lax.div(o, W), 1.0, 0.0).astype(jnp.bfloat16)
 
+    loads[2].wait()
+    loads[3].wait()
     ints = jnp.concatenate([code_ref[...], count_ref[...]], axis=0).astype(f32).astype(jnp.bfloat16)
     apart = jnp.dot(ints, pick(), preferred_element_type=f32)
     for i in range(2 * R):
@@ -196,7 +203,8 @@
         halo_start(*a_args(j))
     halo_start(*o_args)
 
-    ens_copy.wait()
+    loads[4].wait()
+    loads[5].wait()
     for k in range(KM):
         def widen(v, _):
             ensf[k, v] = ens_ref[k, v].astype(f32)
@@ -401,10 +409,15 @@
     back = pl.pallas_call(
         functools.partial(kernel, cfg),
         out_shape=jax.ShapeDtypeStruct((KM, NB, n * R, W), f32),
-        in_specs=[pl.BlockSpec(memory_space=pl.ANY)] + [vmem] * 5,
+        in_specs=[pl.BlockSpec(memory_space=pltpu.HBM)] * 6,
         out_specs=vmem,
         scratch_shapes=[
             pltpu.VMEM((KM, V, NB, n * R, W), jnp.bfloat16),
+            pltpu.VMEM((KM, NB, n * R, W), jnp.bfloat16),
+            pltpu.VMEM(vertical.shape, vertical.dtype),
+            pltpu.VMEM(inverse_var.shape, inverse_var.dtype),
+            pltpu.VMEM(obs_code.shape, obs_code.dtype),
+            pltpu.VMEM(obs_count.shape, obs_count.dtype),
             pltpu.VMEM((KM, V, NB, n * R, W), f32),
             pltpu.VMEM((KM, NB, n * R, W), f32),
             pltpu.VMEM((KC, R + 4, KM, HB, n, W), f32),
@@ -417,7 +430,7 @@
             pltpu.VMEM((KC, R + 4, KM, HB, n, W), f32),
             pltpu.VMEM((2 * R + 4, 8, W), f32),
             pltpu.VMEM((KM, R, NB, n, W), f32),
-            dma,
+            dma((6,)),
             dma((KC, 2)), dma((KC, 2)),
             dma((KC,)), dma((KC,)),
             dma((KC, Q)), dma((KC, Q)),

time: 37.5 us -> 35.4 us (0.944)
  Pallas kernels: 35.7 us -> 33.6 us
    pallas_call x1, Pallas kernels: 35.7 us -> 33.6 us  [per_device(): pl.pallas_call(functools.partial(kernel, cfg), out_shape=jax.ShapeDtypeSt...]
where the time goes in v3:
time: 35.4 us; the launch traced here: 35.3 us
  Pallas kernels  33.6 us (95%)
  other arithmetic  1.68 us (5%)
    pallas_call x1, Pallas kernels, per_device(): pl.pallas_call(functools.partial(kernel, cfg), out_shape=jax.ShapeDtypeSt...  33.6 us
    add x1, other arithmetic, per_device(): return (member_control.astype(f32) + back).reshape(KM, L, R, W)  1.68 us

profile of v3, /device:TPU:0, one launch (start us, length us, event | category | flops | bytes accessed | tf_op | source)
XLA Modules:
  0.0 35.3 jit_solution(14555947519255712721)
XLA Ops:
  0.0 0.0 copy-start
  0.0 33.6 %shard_map.64 = f32[2,16,16,128]{3,2,1,0:T(8,128)} custom-call(bf16[2,4,16,16,128]{4,3,2,1,0:T(8,128)(2,1)} %bitcast.5, bf16[2,16,16,128]{3,2,1,0:T(8,128)(2,1)} %bitcast.6, bf16[128,128]{1,0:T(8,128)(2,1)} %vert_hbm.1, f32[4,128]{1,0:T(4,128)} %ivar_hbm.1, s32[4,256]{1,0:T(4,128)} %code_hbm.1, s32[4,256]{1,0:T(4,128)} %count_hbm.1), custom_call_target="tpu_custom_call" | custom-call | tf_op jit(solution)/shard_map/pallas_call | solution.py:409
  33.6 0.0 copy-done
  33.6 1.7 %convert_add_fusion = f32[2,16,16,128]{3,2,1,0:T(8,128)} fusion(f32[2,16,16,128]{3,2,1,0:T(8,128)} %shard_map.64, bf16[2,16,16,128]{3,2,1,0:T(8,128)(2,1)S(1)} %bitcast.7), kind=kLoop, calls=%fused_computation | loop fusion | flops 131072 | bytes 655360 | tf_op jit(solution)/shard_map/add | solution.py:452
Async XLA Ops:
  0.0 33.6 %copy-start = (bf16[2,128,2,128]{3,2,1,0:T(2,128)(2,1)S(1)}, bf16[2,128,2,128]{3,2,1,0:T(2,128)(2,1)}, u32[]{:S(2)}) copy-start(bf16[2,128,2,128]{3,2,1,0:T(2,128)(2,1)} %param.7) | copy-start | bytes 393220

commit v4 on v3

--- a/solution.py
+++ b/solution.py
@@ -232,7 +232,7 @@
                     part[j, c, pl.ds(q0, group), v, r] = factor * total
             return 0
 
-        lax.fori_loop(0, HB // group, weigh, 0)
+        lax.fori_loop(0, HB // group, weigh, 0, unroll=HB // group <= 4)
         core_copy(j).start()
 
     def stage_join(j):
@@ -242,8 +242,8 @@
             half[j, q] = part[j, core, q] + r1[j, q]
             return 0
 
-        lax.fori_loop(0, Q, join, 0)
-        for d in range(Q - 1, 0, -1):
+        lax.fori_loop(0, Q, join, 0, unroll=Q <= 4)
+        for d in range(1, Q):
             chip_copy(j, d).start()
 
     def stage_reduce(j):
@@ -319,7 +319,7 @@
                          for p in range(2)]
             row = near_weight * (even + odd) + far_weight * (columns(odd, 1) + columns(even, -1))
             adj[j, core, chip, :, r] = row
-        for d in range(Q - 1, 0, -1):
+        for d in range(1, Q):
             gather_copy(j, d).start()
         pass_copy(j, 0).start()
 
@@ -350,7 +350,7 @@
                     proj[j, 2 + r, k, pl.ds(b0, group)] = factor * total
             return 0
 
-        lax.fori_loop(0, HB // group, project, 0)
+        lax.fori_loop(0, HB // group, project, 0, unroll=HB // group <= 4)
         halo_start(*e_args(j))
 
     def stage_settle(j):
@@ -364,7 +364,7 @@
                     rnd[k, r, pl.ds(j * HB + b0, group)] = rows[r]
             return 0
 
-        lax.fori_loop(0, HB // group, settle, 0)
+        lax.fori_loop(0, HB // group, settle, 0, unroll=HB // group <= 4)
 
     stages = (stage_weigh, stage_join, stage_reduce, stage_observe, stage_forward, stage_project, stage_settle)
     for index, j in order_of(KC, len(stages)):

time: 35.4 us -> 35.2 us (level)
  no operation moved by 1% of the time
where the time goes in v4:
time: 35.2 us; the launch traced here: 35 us
  Pallas kernels  33.3 us (95%)
  other arithmetic  1.68 us (5%)
    pallas_call x1, Pallas kernels, per_device(): pl.pallas_call(functools.partial(kernel, cfg), out_shape=jax.ShapeDtypeSt...  33.3 us
    add x1, other arithmetic, per_device(): return (member_control.astype(f32) + back).reshape(KM, L, R, W)  1.68 us

profile of v4, /device:TPU:0, one launch (start us, length us, event | category | flops | bytes accessed | tf_op | source)
XLA Modules:
  0.0 35.0 jit_solution(15831538306813606286)
XLA Ops:
  0.0 0.0 copy-start
  0.0 33.3 %shard_map.64 = f32[2,16,16,128]{3,2,1,0:T(8,128)} custom-call(bf16[2,4,16,16,128]{4,3,2,1,0:T(8,128)(2,1)} %bitcast.5, bf16[2,16,16,128]{3,2,1,0:T(8,128)(2,1)} %bitcast.6, bf16[128,128]{1,0:T(8,128)(2,1)} %vert_hbm.1, f32[4,128]{1,0:T(4,128)} %ivar_hbm.1, s32[4,256]{1,0:T(4,128)} %code_hbm.1, s32[4,256]{1,0:T(4,128)} %count_hbm.1), custom_call_target="tpu_custom_call" | custom-call | tf_op jit(solution)/shard_map/pallas_call | solution.py:409
  33.4 0.0 copy-done
  33.4 1.7 %convert_add_fusion = f32[2,16,16,128]{3,2,1,0:T(8,128)} fusion(f32[2,16,16,128]{3,2,1,0:T(8,128)} %shard_map.64, bf16[2,16,16,128]{3,2,1,0:T(8,128)(2,1)S(1)} %bitcast.7), kind=kLoop, calls=%fused_computation | loop fusion | flops 131072 | bytes 655360 | tf_op jit(solution)/shard_map/add | solution.py:452
Async XLA Ops:
  0.0 33.4 %copy-start = (bf16[2,128,2,128]{3,2,1,0:T(2,128)(2,1)S(1)}, bf16[2,128,2,128]{3,2,1,0:T(2,128)(2,1)}, u32[]{:S(2)}) copy-start(bf16[2,128,2,128]{3,2,1,0:T(2,128)(2,1)} %param.7) | copy-start | bytes 393220
